TPU v7x, 32 devices: a whole 2x2x4 slice. The times are simulated.
32 devices in a mesh: grp: 2 (over y), seq: 16 (over z, x, core).
Axes of the slice: x: 2, y: 2, z: 4, core: 2. Of those that a mesh axis runs over, the one named last changes fastest.
Arguments:
- queries: bfloat16 [8192, 2048], P(('grp', 'seq')), parts along dimension 0, may hold values from -6 to 6
- keys: bfloat16 [8192, 2048], P(('grp', 'seq')), parts along dimension 0, may hold values from -6 to 6
- values: bfloat16 [8192, 2048], P(('grp', 'seq')), parts along dimension 0, may hold values from -6 to 6
- level_index: int32 [8192], P(('grp', 'seq')), parts along dimension 0, may hold values from 0 to 63
- level_table: float32 [64, 18, 16], replicated, may hold values from 0 to 10
- norm_gain: float32 [2048], replicated, may hold values from 0.1 to 1.9
- out_weight: bfloat16 [2048, 2048], P(None, 'seq'), may hold values from -0.125 to 0.125
Outputs:
- block_out: bfloat16 [8192, 2048], P(('grp', 'seq')), parts along dimension 0
There are 2 independent parts, one for each index of `grp`. A program takes and returns all parts, laid end to end along the dimension named above; an argument that names none is the same for every part. Nothing has to cross between parts.
All inputs are finite; a program needn't handle non-finite values.
Results may differ from a plain program's by a relative error of at most 0.0057.
Values may be sent and summed in bfloat16 or wider, within the bound.
A program may use at most 128 MiB of HBM per device.

v0:
```python
import math

import jax
import jax.numpy as jnp
from jax import lax
from jax.sharding import PartitionSpec as P


def from_partner(block, axis, apart):
    count = lax.axis_size(axis)
    route = []
    for low in range(count):
        high = low | 1 << apart
        if high != low and high < count:
            route += [(low, high), (high, low)]
    return lax.ppermute(block, axis, route)


def body(queries, keys, values, level_index, level_table, norm_gain, out_weight):
    stretch, width = queries.shape
    table_rows, level_count, heads = level_table.shape
    head_dim = width // heads
    scale = 1.0 / math.sqrt(head_dim)
    log_stretch = stretch.bit_length() - 1
    log_blocks = lax.axis_size("seq").bit_length() - 1
    rank = lax.axis_index("seq")
    q_heads = jnp.transpose(queries.reshape(stretch, heads, head_dim), (1, 0, 2))
    k_heads = jnp.transpose(keys.reshape(stretch, heads, head_dim), (1, 0, 2))
    v_heads = jnp.transpose(values.reshape(stretch, heads, head_dim), (1, 0, 2))
    selector = (level_index[:, None] == jnp.arange(table_rows, dtype=jnp.int32)[None, :]).astype(
        jnp.float32
    )
    lam = jnp.dot(
        selector,
        level_table.reshape(table_rows, level_count * heads),
        precision=lax.Precision.HIGHEST,
    )
    lam_heads = jnp.transpose(lam.reshape(stretch, level_count, heads), (2, 0, 1))
    state = jnp.einsum("hse,hsf->hef", k_heads, v_heads, preferred_element_type=jnp.float32)
    positions = jnp.arange(stretch, dtype=jnp.int32)
    level_grid = jnp.zeros((positions.shape[0], positions.shape[0]), jnp.int32)
    for bit in range(log_stretch):
        level_grid = level_grid + (
            jnp.right_shift(positions[:, None], bit) != jnp.right_shift(positions[None, :], bit)
        ).astype(jnp.int32)
    scores = (
        jnp.einsum("hte,hse->hts", q_heads, k_heads, preferred_element_type=jnp.float32) * scale
    )
    picked = jnp.zeros_like(scores)
    for level in range(log_stretch + 1):
        picked = jnp.where((level_grid == level)[None], lam_heads[:, :, level : level + 1], picked)
    weighted = jnp.where(
        (positions[None, :] <= positions[:, None])[None], picked * scores, 0.0
    ).astype(jnp.bfloat16)
    pieces = jnp.einsum("hts,hsf->htf", weighted, v_heads, preferred_element_type=jnp.float32)
    group = state
    far = jnp.zeros((heads, stretch, head_dim), jnp.float32)
    for bit in range(log_blocks):
        owned = jnp.right_shift(rank, bit) % 2 == 1
        other = from_partner(group, "seq", bit)
        bucket = other.astype(jnp.bfloat16)
        term = jnp.einsum("hte,hef->htf", q_heads, bucket, preferred_element_type=jnp.float32)
        weight = lam_heads[:, :, log_stretch + 1 + bit : log_stretch + 2 + bit]
        far = far + jnp.where(owned, weight * term * scale, 0.0)
        if bit + 1 < log_blocks:
            group = group + other
    mixed = pieces + far
    normed = (
        mixed
        * lax.rsqrt(jnp.mean(mixed * mixed, axis=2, keepdims=True) + 1e-06)
        * norm_gain.reshape(heads, 1, head_dim)
    )
    normed = jnp.transpose(normed, (1, 0, 2)).reshape(stretch, width).astype(jnp.bfloat16)
    full_weight = lax.all_gather(out_weight, "seq", axis=1, tiled=True)
    return jnp.dot(normed, full_weight, preferred_element_type=jnp.float32).astype(jnp.bfloat16)


def solution(mesh):
    placed = (
        P(("grp", "seq"), None),
        P(("grp", "seq"), None),
        P(("grp", "seq"), None),
        P(("grp", "seq")),
        P(),
        P(),
        P(None, "seq"),
    )
    return jax.shard_map(
        body, mesh=mesh, in_specs=placed, out_specs=P(("grp", "seq"), None), check_vma=False
    )
```

profile of v0, /device:TPU:0, one launch (start us, length us, event | category | flops | bytes accessed | tf_op | source)
XLA Modules:
  0.0 159.4 jit_solution(18002641853276145586)
XLA Ops:
  6.5 0.7 all-gather.2.cloned.1.call-update
  7.3 1.5 copy.30
  9.2 0.6 collective-permute-start
  9.8 0.6 iota_shift-right-arithmetic_fusion
  10.4 0.5 iota_shift-right-arithmetic_fusion.2
  11.4 0.7 collective-permute-done
  12.2 2.9 %collective-permute-start.1 = (f32[16,128,128]{2,1,0:T(8,128)S(1)}, f32[16,128,128]{2,1,0:T(8,128)S(1)}, u32[]{:S(2)}, u32[]{:S(2)}) collective-permute-start(f32[16,128,128]{2,1,0:T(8,128)S(1)} %add.400), channel_id=1, source_target_pairs={{0,2},{2,0},{1,3},{3,1},{4,6},{6,4},{5,7},{7,5},{8,10},{10,8},{9,1... | collective-permute-start | bytes 3145736 | tf_op jit(solution)/shard_map/ppermute | solution.py:16
  15.1 0.5 iota_shift-right-arithmetic_fusion.4
  15.7 0.7 iota_compare_fusion
  16.3 0.6 copy_bitcast_fusion
  16.9 0.6 copy_bitcast_fusion.2
  17.5 0.6 copy_bitcast_fusion.4
  18.2 0.6 copy_bitcast_fusion.6
  18.8 25.4 %collective-permute-done.1 = f32[16,128,128]{2,1,0:T(8,128)S(1)} collective-permute-done((f32[16,128,128]{2,1,0:T(8,128)S(1)}, f32[16,128,128]{2,1,0:T(8,128)S(1)}, u32[]{:S(2)}, u32[]{:S(2)}) %collective-permute-start.1) | collective-permute-done | bytes 1048608 | tf_op jit(solution)/shard_map/ppermute | solution.py:16
  44.4 1.9 %collective-permute-start.2 = (f32[16,128,128]{2,1,0:T(8,128)S(1)}, f32[16,128,128]{2,1,0:T(8,128)}, u32[]{:S(2)}, u32[]{:S(2)}) collective-permute-start(f32[16,128,128]{2,1,0:T(8,128)S(1)} %add.403), channel_id=1, source_target_pairs={{0,4},{4,0},{1,5},{5,1},{2,6},{6,2},{3,7},{7,3},{8,12},{12,8},{9,1... | collective-permute-start | bytes 3145736 | tf_op jit(solution)/shard_map/ppermute | solution.py:16
  46.2 0.6 iota_shift-right-arithmetic_fusion.6
  46.8 1.2 copy.48
  48.0 0.6 copy_bitcast_fusion.9
  48.6 0.6 copy_bitcast_fusion.11
  49.3 2.2 %broadcast_compare_fusion.8 = (pred[256,256]{1,0:T(8,128)(4,1)S(1)}, pred[256,256]{1,0:T(8,128)(4,1)S(1)}, pred[256,256]{1,0:T(8,128)(4,1)S(1)}, pred[256,256]{1...) fusion(s32[256]{0:T(256)} %get-tuple-element.48, ...), kind=kLoop, calls=%fused_computation.55 | loop fusion | flops 2097152 | bytes 598016 | tf_op jit(solution)/shard_map/eq | solution.py:51
  51.5 1.8 %fusion.23 = f32[16,128,256]{2,1,0:T(8,128)} fusion(f32[16,128,128]{2,1,0:T(8,128)S(1)} %copy-done.4, bf16[256,2048]{1,0:T(8,128)(2,1)S(1)} %copy-done), kind=kOutput, calls=%fused_computation.33 | convolution fusion | flops 134479872 | bytes 4194304 | tf_op jit(solution)/shard_map/hte,hef->htf/dot_general | solution.py:62
  53.3 43.4 %collective-permute-done.2 = f32[16,128,128]{2,1,0:T(8,128)} collective-permute-done((f32[16,128,128]{2,1,0:T(8,128)S(1)}, f32[16,128,128]{2,1,0:T(8,128)}, u32[]{:S(2)}, u32[]{:S(2)}) %collective-permute-start.2) | collective-permute-done | bytes 1048608 | tf_op jit(solution)/shard_map/ppermute | solution.py:16
  96.7 1.3 add.406
  98.1 1.0 collective-permute-start.3
  99.1 1.8 %fusion.22 = f32[16,128,256]{2,1,0:T(8,128)} fusion(f32[16,128,128]{2,1,0:T(8,128)S(1)} %copy-done.6, bf16[256,2048]{1,0:T(8,128)(2,1)S(1)} %copy-done), kind=kOutput, calls=%fused_computation.32 | convolution fusion | flops 134479872 | bytes 4194304 | tf_op jit(solution)/shard_map/hte,hef->htf/dot_general | solution.py:62
  100.9 3.1 %fusion.21 = f32[16,128,256]{2,1,0:T(8,128)} fusion(f32[16,128,128]{2,1,0:T(8,128)} %collective-permute-done.2, bf16[256,2048]{1,0:T(8,128)(2,1)S(1)} %copy-done), kind=kOutput, calls=%fused_computation.31 | convolution fusion | flops 134479872 | bytes 4194304 | tf_op jit(solution)/shard_map/hte,hef->htf/dot_general | solution.py:62
  104.0 24.7 %collective-permute-done.3 = bf16[16,128,128]{2,1,0:T(8,128)(2,1)S(1)} collective-permute-done((bf16[16,128,128]{2,1,0:T(8,128)(2,1)S(1)}, bf16[16,128,128]{2,1,0:T(8,128)(2,1)S(1)}, u32[]{:S(2)}, u32[]{:S(2)}) %collective-permute-start.3) | collective-permute-done | bytes 524320 | tf_op jit(solution)/shard_map/ppermute | solution.py:16
  128.7 0.5 fusion.20
  129.2 10.6 %fusion.1 = (f32[16,256]{1,0:T(8,128)}, f32[16,256,128]{1,2,0:T(8,128)}) fusion(f32[16,128,256]{2,1,0:T(8,128)S(1)} %fusion.20, f32[16,128,256]{2,1,0:T(8,128)} %fusion.21, f32[16,128,256]{2,1,0:T(8,128)} %fusion.22, f32[16,128,256]{2,1,0:T(8,128)} %fusion.23, f32[16,256]{1,0:T(8,128)S(1)} %get-tuple-element.25, f32[16,256]{1,0:T(8,128)} %get-tuple-element.23, ...), kind=kOutput, calls=%fused_computation.4 | convolution fusion | flops 559935488 | bytes 14516228 | tf_op jit(solution)/shard_map/hts,hsf->htf/dot_general | solution.py:55
  139.8 0.7 rsqrt_bitcast_fusion
  140.5 5.0 %fusion.8 = bf16[256,16,128]{0,2,1:T(8,128)(2,1)} fusion(f32[16,128,256]{2,1,0:T(8,128)S(1)} %fusion.20, f32[16,128,256]{2,1,0:T(8,128)} %fusion.21, f32[16,128,256]{2,1,0:T(8,128)} %fusion.22, f32[16,128,256]{2,1,0:T(8,128)} %fusion.23, f32[16,256,128]{1,2,0:T(8,128)} %get-tuple-element.36, f32[16,128]{1,0:T(8,128)} %bitcast.172, ...), kind=kLoop, calls=%fused_computation.12 | loop fusion | flops 9961472 | bytes 11624452 | tf_op jit(solution)/shard_map/convert_element_type | solution.py:73
  145.6 7.0 %convolution_convert_fusion = bf16[256,2048]{1,0:T(8,128)(2,1)} fusion(bf16[256,2048]{0,1:T(8,128)(2,1)} %bitcast.164, bf16[2048,2048]{1,0:T(8,128)(2,1)} %all-gather.2.cloned.1.call-done), kind=kOutput, calls=%fused_computation.1 | convolution fusion | flops 2148007936 | bytes 10485760 | tf_op jit(solution)/shard_map/dot_general | solution.py:75
  (30 shorter events, 1.2 us)
Async XLA Ops:
  6.5 45.0 %copy-start = (bf16[256,2048]{1,0:T(8,128)(2,1)S(1)}, bf16[256,2048]{1,0:T(8,128)(2,1)}, u32[]{:S(2)}) copy-start(bf16[256,2048]{1,0:T(8,128)(2,1)} %param.7) | copy-start | bytes 3145732
  6.5 2.2 %copy-start.1 = (bf16[256,2048]{1,0:T(8,128)(2,1)S(1)}, bf16[256,2048]{1,0:T(8,128)(2,1)}, u32[]{:S(2)}) copy-start(bf16[256,2048]{1,0:T(8,128)(2,1)} %param.9) | copy-start | bytes 3145732
  6.5 139.0 %all-gather.2.cloned.1.call-start = ((), (), s32[]{:S(2)}) async-start(), calls=%async_computation | async-start | bytes 8912896 | tf_op jit(solution)/shard_map/all_gather | solution.py:74
  8.7 3.5 %copy-start.2 = (bf16[256,2048]{0,1:T(8,128)(2,1)}, bf16[256,2048]{0,1:T(8,128)(2,1)S(1)}, u32[]{:S(2)}) copy-start(bf16[256,2048]{0,1:T(8,128)(2,1)S(1)} %copy.30) | copy-start | bytes 3145732
  8.8 2.2 %copy-start.7 = (f32[64,18,16]{0,2,1:T(8,128)S(1)}, f32[64,18,16]{0,2,1:T(8,128)}, u32[]{:S(2)}) copy-start(f32[64,18,16]{0,2,1:T(8,128)} %param.11) | copy-start | bytes 221188
  8.8 2.1 %copy-start.10 = (s32[256]{0:T(256)S(1)}, s32[256]{0:T(256)}, u32[]{:S(2)}) copy-start(s32[256]{0:T(256)} %param.10) | copy-start | bytes 3076
  9.2 2.8 %collective-permute-start = (f32[16,128,128]{2,1,0:T(8,128)S(1)}, f32[16,128,128]{2,1,0:T(8,128)S(1)}, u32[]{:S(2)}, u32[]{:S(2)}) collective-permute-start(f32[16,128,128]{2,1,0:T(8,128)S(1)} %fusion.18), channel_id=1, source_target_pairs={{0,1},{1,0},{2,3},{3,2},{4,5},{5,4},{6,7},{7,6},{8,9},{9,8},{10,11... | collective-permute-start | bytes 3145736 | tf_op jit(solution)/shard_map/ppermute | solution.py:16
  12.1 32.3 %copy-start.3 = (f32[16,128,128]{2,1,0:T(8,128)}, f32[16,128,128]{2,1,0:T(8,128)S(1)}, u32[]{:S(2)}) copy-start(f32[16,128,128]{2,1,0:T(8,128)S(1)} %collective-permute-done) | copy-start | bytes 3145732
  12.2 32.0 %collective-permute-start.1 = (f32[16,128,128]{2,1,0:T(8,128)S(1)}, f32[16,128,128]{2,1,0:T(8,128)S(1)}, u32[]{:S(2)}, u32[]{:S(2)}) collective-permute-start(f32[16,128,128]{2,1,0:T(8,128)S(1)} %add.400), channel_id=1, source_target_pairs={{0,2},{2,0},{1,3},{3,1},{4,6},{6,4},{5,7},{7,5},{8,10},{10,8},{9,1... | collective-permute-start | bytes 3145736 | tf_op jit(solution)/shard_map/ppermute | solution.py:16
  44.2 2.0 %copy-start.5 = (f32[16,128,128]{2,1,0:T(8,128)}, f32[16,128,128]{2,1,0:T(8,128)S(1)}, u32[]{:S(2)}) copy-start(f32[16,128,128]{2,1,0:T(8,128)S(1)} %collective-permute-done.1) | copy-start | bytes 3145732
  44.4 52.4 %collective-permute-start.2 = (f32[16,128,128]{2,1,0:T(8,128)S(1)}, f32[16,128,128]{2,1,0:T(8,128)}, u32[]{:S(2)}, u32[]{:S(2)}) collective-permute-start(f32[16,128,128]{2,1,0:T(8,128)S(1)} %add.403), channel_id=1, source_target_pairs={{0,4},{4,0},{1,5},{5,1},{2,6},{6,2},{3,7},{7,3},{8,12},{12,8},{9,1... | collective-permute-start | bytes 3145736 | tf_op jit(solution)/shard_map/ppermute | solution.py:16
  46.8 2.4 %copy-start.8 = (s32[256]{0:T(256)S(1)}, s32[256]{0:T(256)}, u32[]{:S(2)}) copy-start(s32[256]{0:T(256)} %get-tuple-element.54) | copy-start | bytes 3076
  46.8 2.4 %copy-start.9 = (s32[256]{0:T(256)S(1)}, s32[256]{0:T(256)}, u32[]{:S(2)}) copy-start(s32[256]{0:T(256)} %get-tuple-element.55) | copy-start | bytes 3076
  46.8 4.7 %copy-start.4 = (f32[16,128,128]{2,1,0:T(8,128)S(1)}, f32[16,128,128]{2,1,0:T(8,128)}, u32[]{:S(2)}) copy-start(f32[16,128,128]{2,1,0:T(8,128)} %copy-done.3) | copy-start | bytes 3145732
  53.3 45.8 %copy-start.6 = (f32[16,128,128]{2,1,0:T(8,128)S(1)}, f32[16,128,128]{2,1,0:T(8,128)}, u32[]{:S(2)}) copy-start(f32[16,128,128]{2,1,0:T(8,128)} %copy-done.5) | copy-start | bytes 3145732
  98.1 30.6 %collective-permute-start.3 = (bf16[16,128,128]{2,1,0:T(8,128)(2,1)S(1)}, bf16[16,128,128]{2,1,0:T(8,128)(2,1)S(1)}, u32[]{:S(2)}, u32[]{:S(2)}) collective-permute-start(bf16[16,128,128]{2,1,0:T(8,128)(2,1)S(1)} %add.406), channel_id=1, source_target_pairs={{0,8},{8,0},{1,9},{9,1},{2,10},{10,2},{3,11},{11,3},{4,12},{12,4},... | collective-permute-start | bytes 1572872 | tf_op jit(solution)/shard_map/ppermute | solution.py:16
Sparse Core Ops, SparseCore 0:
  9.5 116.5 all-gather.1
where the time goes:
time: 160 us; the launch traced here: 159 us
  waiting for transfers between devices  94.9 us (59%)
  matrix products  25.6 us (16%)
  between operations  13.5 us (8%)
  other arithmetic  12.5 us (8%)
  local copies, waits for them, and re-layouts  6.56 us (4%)
  starting transfers between devices  6.37 us (4%)
    ppermute x4, waiting for transfers between devices, from_partner(): return lax.ppermute(block, axis, route)  94.2 us
    dot_general x1, matrix products, body(): jnp.einsum('hts,hsf->htf', weighted, v_heads, preferred_element_type=jnp....  10.6 us
    dot_general x4, matrix products, body(): jnp.einsum('hte,hef->htf', q_heads, bucket, preferred_element_type=jnp.fl...  7.23 us
    dot_general x1, matrix products, body(): jnp.dot(normed, full_weight, preferred_element_type=jnp.float32)  7.04 us
    ppermute x4, starting transfers between devices, from_partner(): return lax.ppermute(block, axis, route)  6.37 us
    convert_element_type x1, other arithmetic, body(): jnp.transpose(normed, (1, 0, 2)).reshape(stretch, width)  5.02 us
    unnamed x28, local copies, waits for them, and re-layouts  3.69 us
  transfers between devices with their start and end apart: 5, of which 4 were waited for; matrix products, arithmetic and copies ran while one was open for 24% of the time, Pallas kernels for 0%

commit v1 on v0

--- a/solution.py
+++ b/solution.py
@@ -1,9 +1,16 @@
+import functools
 import math
 
 import jax
 import jax.numpy as jnp
 from jax import lax
+from jax.experimental import pallas as pl
+from jax.experimental.pallas import tpu as pltpu
 from jax.sharding import PartitionSpec as P
+
+MESH = pl.DeviceIdType.MESH
+UP, DOWN, ACROSS, OTHER, CORE = range(5)
+ST, XQ, B1C, ZQ, B2C, ZS, B3C = range(7)
 
 
 def from_partner(block, axis, apart):
@@ -16,7 +23,7 @@
     return lax.ppermute(block, axis, route)
 
 
-def body(queries, keys, values, level_index, level_table, norm_gain, out_weight):
+def plain_body(queries, keys, values, level_index, level_table, norm_gain, out_weight):
     stretch, width = queries.shape
     table_rows, level_count, heads = level_table.shape
     head_dim = width // heads
@@ -75,6 +82,500 @@
     return jnp.dot(normed, full_weight, preferred_element_type=jnp.float32).astype(jnp.bfloat16)
 
 
+def kernel(
+    dims,
+    q_hbm, k_hbm, v_hbm, idx_ref, tab_ref, gain_ref, w_hbm, out_ref,
+    q, k, v, wbuf, st, st_bf, b0, b1, b2, b3, ps, ps_bf, quad, quad_bf, mixed, normed, lam,
+    load_sem, w_send, w_recv, s_send, s_recv,
+):
+    count, ways, part = dims
+    stretch, width = q.shape
+    heads, table_rows, level_count = tab_ref.shape
+    head_dim = width // heads
+    half = heads // 2
+    piece = half // 2
+    scale = 1.0 / math.sqrt(head_dim)
+    log_stretch = stretch.bit_length() - 1
+    mid = stretch // 2
+    layers = count // (2 * ways)
+    rows, cols = w_hbm.shape
+
+    y = lax.axis_index("grp")
+    r = lax.axis_index("seq")
+    c = lax.rem(r, 2)
+    x = lax.rem(r // 2, 2)
+    z = r // 4
+    to_core = (y, r + 1 - 2 * c)
+    to_x = (y, r + 2 - 4 * x)
+    to_y = (1 - y, r)
+    to_up = (y, r + 4)
+    to_down = (y, r - 4)
+    mine = c * half
+    has_up = z < layers - 1
+    has_down = z > 0
+
+    barrier = pltpu.get_barrier_semaphore()
+
+    def greet(device):
+        pl.semaphore_signal(barrier, inc=1, device_id=device, device_id_type=MESH)
+
+    def wait_n(n):
+        pl.semaphore_wait(barrier, n)
+
+    greet(to_core)
+    greet(to_x)
+    greet(to_y)
+    pl.when(has_up)(lambda: greet(to_up))
+    pl.when(has_down)(lambda: greet(to_down))
+
+    def load(i, src, dst):
+        return pltpu.make_async_copy(src, dst, load_sem.at[i])
+
+    loads = [
+        load(0, k_hbm, k), load(1, v_hbm, v), load(2, q_hbm, q), load(3, w_hbm, wbuf.at[r]),
+    ]
+    for one in loads:
+        one.start()
+    pl.semaphore_wait(
+        barrier, 3 + jnp.where(has_up, 1, 0) + jnp.where(has_down, 1, 0)
+    )
+
+    Y, C, O = "y", "c", "o"
+
+    def chunk_rows(which):
+        if which == C:
+            return pl.ds(part, rows - 2 * part)
+        side = y if which == Y else 1 - y
+        return pl.ds(pl.multiple_of(side * (rows - part), 128), part)
+
+    def chunk_id(which):
+        if which == C:
+            return 1
+        return 2 * y if which == Y else 2 * (1 - y)
+
+    targets = {UP: to_up, DOWN: to_down, ACROSS: to_x, OTHER: to_y, CORE: to_core}
+
+    def w_copy(shard, which, way, own=False):
+        at = chunk_rows(which)
+        spot = wbuf.at[shard, at]
+        return pltpu.make_async_remote_copy(
+            src_ref=w_hbm.at[at] if own else spot,
+            dst_ref=spot,
+            send_sem=w_send.at[way, shard // 2, chunk_id(which)],
+            recv_sem=w_recv.at[shard, chunk_id(which)],
+            device_id=targets[way],
+            device_id_type=MESH,
+        )
+
+    def shard_of(zz, xx, cc):
+        return zz * 4 + xx * 2 + cc
+
+    sent = []
+
+    def send(cond, shard, which, way, own=False):
+        def go():
+            w_copy(shard, which, way, own).start()
+
+        if cond is None:
+            go()
+        else:
+            pl.when(cond)(go)
+        sent.append((cond, shard, which, way, own))
+
+    def both(a, b):
+        return b if a is None else jnp.logical_and(a, b)
+
+    def under(cond, go):
+        if cond is None:
+            go()
+        else:
+            pl.when(cond)(go)
+
+    def arrive(cond, shard, which, way):
+        under(cond, lambda: w_copy(shard, which, way).wait_recv())
+
+    for which in (Y, C):
+        send(has_up, r, which, UP, True)
+        send(has_down, r, which, DOWN, True)
+    send(None, r, Y, ACROSS, True)
+    for which in (Y, C, O):
+        send(None, r, which, CORE, True)
+
+    def from_line(d, side, which):
+        zz = z - d if side == UP else z + d
+        ok = z >= d if side == UP else z + d < layers
+        shard = shard_of(jnp.where(ok, zz, z), x, c)
+        arrive(ok, shard, which, side)
+        send(both(ok, has_up if side == UP else has_down), shard, which, side)
+        send(ok, shard, which, ACROSS)
+        if which == Y:
+            send(ok, shard, which, OTHER)
+        send(ok, shard, which, CORE)
+
+    def from_across(d, side, which):
+        if d == 0:
+            ok, zz = None, z
+        else:
+            ok = z >= d if side == UP else z + d < layers
+            zz = jnp.where(ok, z - d if side == UP else z + d, z)
+        shard = shard_of(zz, 1 - x, c)
+        arrive(ok, shard, which, ACROSS)
+        if which == Y:
+            send(ok, shard, which, OTHER)
+        send(ok, shard, which, CORE)
+
+    def from_other(d, side, across):
+        if d == 0:
+            ok, zz = None, z
+        else:
+            ok = z >= d if side == UP else z + d < layers
+            zz = jnp.where(ok, z - d if side == UP else z + d, z)
+        shard = shard_of(zz, 1 - x if across else x, c)
+        arrive(ok, shard, O, OTHER)
+        send(ok, shard, O, CORE)
+
+    def line(d):
+        for which in (Y, C):
+            for side in (UP, DOWN):
+                from_line(d, side, which)
+
+    def across(d, which):
+        for side in (UP,) if d == 0 else (UP, DOWN):
+            from_across(d, side, which)
+
+    def other(d, far_side):
+        for side in (UP,) if d == 0 else (UP, DOWN):
+            from_other(d, side, far_side)
+
+    s_sent = []
+
+    def s_copy(kind, n, src, dst, to):
+        return pltpu.make_async_remote_copy(
+            src_ref=src, dst_ref=dst, send_sem=s_send.at[kind, n], recv_sem=s_recv.at[kind, n],
+            device_id=to, device_id_type=MESH,
+        )
+
+    def s_start(cond, *args):
+        under(cond, lambda: s_copy(*args).start())
+        s_sent.append((cond, args))
+
+    def heads_at(start, n):
+        return pl.ds(start, n)
+
+    def lanes(h):
+        return pl.ds(pl.multiple_of(h * head_dim, head_dim), head_dim)
+
+    loads[0].wait()
+    loads[1].wait()
+
+    def state_loop(first):
+        def step(i, _):
+            for u in range(2):
+                h = first + i * 2 + u
+                one = lax.dot_general(
+                    k[:, lanes(h)], v[:, lanes(h)], (((0,), (0,)), ((), ())),
+                    preferred_element_type=jnp.float32,
+                )
+                st[h] = one
+                st_bf[h] = one.astype(jnp.bfloat16)
+            return 0
+
+        lax.fori_loop(0, half // 2, step, 0)
+
+    state_loop(0)
+    s_start(None, ST, 0, st_bf.at[pl.ds(0, half)], b0.at[pl.ds(0, half)], to_core)
+    state_loop(half)
+    s_start(c == 0, ST, 1, st_bf.at[pl.ds(half, half)], b0.at[pl.ds(half, half)], to_core)
+
+    row_of = lax.broadcasted_iota(jnp.int32, (table_rows, stretch), 0)
+    onehot_t = jnp.where(row_of == idx_ref[...], 1.0, 0.0)
+    onehot = jnp.transpose(onehot_t, (1, 0)).astype(jnp.bfloat16)
+
+    def lam_step(h, _):
+        full = tab_ref[h]
+        hi = full.astype(jnp.bfloat16)
+        rest = full - hi.astype(jnp.float32)
+        mi = rest.astype(jnp.bfloat16)
+        lo = (rest - mi.astype(jnp.float32)).astype(jnp.bfloat16)
+        total = jnp.dot(onehot, lo, preferred_element_type=jnp.float32)
+        total = total + jnp.dot(onehot, mi, preferred_element_type=jnp.float32)
+        total = total + jnp.dot(onehot, hi, preferred_element_type=jnp.float32)
+        lam[h, :, pl.ds(0, level_count)] = total
+        return 0
+
+    lax.fori_loop(0, heads, lam_step, 0)
+
+    ti = lax.broadcasted_iota(jnp.int32, (mid, mid), 0)
+    si = lax.broadcasted_iota(jnp.int32, (mid, mid), 1)
+    grid = jnp.zeros((mid, mid), jnp.int32)
+    for bit in range(log_stretch - 1):
+        grid = grid + jnp.where(
+            jnp.right_shift(ti, bit) != jnp.right_shift(si, bit), 1, 0
+        )
+    grid = jnp.where(si <= ti, grid, -1)
+
+    def local(first, last):
+        loads_done = first == 0
+        if loads_done:
+            loads[2].wait()
+
+        def step(i, _):
+            for u in range(2):
+                h = first + i * 2 + u
+                qh, kh, vh = q[:, lanes(h)], k[:, lanes(h)], v[:, lanes(h)]
+                s = lax.dot_general(
+                    qh, kh, (((1,), (1,)), ((), ())), preferred_element_type=jnp.float32
+                ) * scale
+                weight = lam[h]
+
+                def pick(w):
+                    out = jnp.zeros((mid, mid), jnp.float32)
+                    for level in range(log_stretch):
+                        out = jnp.where(grid == level, w[:, level : level + 1], out)
+                    return out
+
+                low, high = weight[:mid], weight[mid:]
+                p00 = (pick(low) * s[:mid, :mid]).astype(jnp.bfloat16)
+                p10 = (high[:, log_stretch : log_stretch + 1] * s[mid:, :mid]).astype(jnp.bfloat16)
+                p11 = (pick(high) * s[mid:, mid:]).astype(jnp.bfloat16)
+                mixed[pl.ds(0, mid), lanes(h)] = jnp.dot(
+                    p00, vh[:mid], preferred_element_type=jnp.float32
+                )
+                mixed[pl.ds(mid, mid), lanes(h)] = jnp.dot(
+                    jnp.concatenate([p10, p11], axis=1), vh, preferred_element_type=jnp.float32
+                )
+            return 0
+
+        lax.fori_loop(0, (last - first) // 2, step, 0)
+
+    def far(bit, bucket):
+        def step(i, _):
+            for u in range(2):
+                h = i * 2 + u
+                term = jnp.dot(q[:, lanes(h)], bucket[h], preferred_element_type=jnp.float32)
+                level = log_stretch + 1 + bit
+                weight = lam[h][:, level : level + 1]
+                mixed[:, lanes(h)] = mixed[:, lanes(h)] + weight * term * scale
+            return 0
+
+        lax.fori_loop(0, heads // 2, step, 0)
+
+    def own(n):
+        return pl.ds(mine + n * piece, piece)
+
+    def chip_sum():
+        pl.when(c == 0)(lambda: s_copy(ST, 0, st_bf.at[pl.ds(0, half)], b0.at[pl.ds(0, half)], to_core).wait_recv())
+        pl.when(c == 1)(lambda: s_copy(ST, 1, st_bf.at[pl.ds(half, half)], b0.at[pl.ds(half, half)], to_core).wait_recv())
+        for n in range(2):
+            def step(i, _, n=n):
+                h = n * piece + i
+                one = st[mine + h] + b0[mine + h].astype(jnp.float32)
+                ps[h] = one
+                ps_bf[h] = one.astype(jnp.bfloat16)
+                return 0
+
+            lax.fori_loop(0, piece, step, 0)
+            s_start(None, XQ, n, ps_bf.at[pl.ds(n * piece, piece)], b1.at[own(n)], to_x)
+
+    def quad_sum():
+        even = lax.rem(z, 2) == 0
+        for n in range(2):
+            s_copy(XQ, n, ps_bf.at[pl.ds(n * piece, piece)], b1.at[own(n)], to_x).wait_recv()
+            s_start(x == 1, B1C, n, b1.at[own(n)], b1.at[own(n)], to_core)
+
+            def step(i, _, n=n):
+                h = n * piece + i
+                one = ps[h] + b1[mine + h].astype(jnp.float32)
+                quad[h] = one
+                quad_bf[h] = one.astype(jnp.bfloat16)
+                return 0
+
+            lax.fori_loop(0, piece, step, 0)
+            s_start(even, ZQ, n, quad_bf.at[pl.ds(n * piece, piece)], b2.at[own(n)], to_up)
+
+    def layer_sum():
+        odd = lax.rem(z, 2) == 1
+        for n in range(2):
+            at = pl.ds(n * piece, piece)
+            pl.when(odd)(lambda: s_copy(ZQ, n, quad_bf.at[at], b2.at[own(n)], to_down).wait_recv())
+            s_start(odd, B2C, n, b2.at[own(n)], b2.at[own(n)], to_core)
+
+            def sums(n=n):
+                def step(i, _):
+                    h = n * piece + i
+                    ps_bf2[h] = (quad[h] + b2[mine + h].astype(jnp.float32)).astype(jnp.bfloat16)
+                    return 0
+
+                lax.fori_loop(0, piece, step, 0)
+
+            pl.when(z == 1)(sums)
+            s_start(z == 1, ZS, n, ps_bf2.at[at], b3.at[own(n)], to_up)
+
+    ps_bf2 = quad_bf
+
+    def top_sum():
+        for n in range(2):
+            pl.when(z >= 2)(lambda: s_copy(ZS, n, b3.at[own(n)], b3.at[own(n)], to_down).wait_recv())
+            s_start(z == 2, ZS, n, b3.at[own(n)], b3.at[own(n)], to_up)
+            s_start(z >= 2, B3C, n, b3.at[own(n)], b3.at[own(n)], to_core)
+
+    def theirs(n):
+        return pl.ds(half - mine + n * piece, piece)
+
+    def from_core(kind, buf):
+        for n in range(2):
+            s_copy(kind, n, buf.at[theirs(n)], buf.at[theirs(n)], to_core).wait_recv()
+
+    chip_sum()
+    send(None, r, C, ACROSS, True)
+    local(0, 4)
+    line(1)
+    across(0, Y)
+    quad_sum()
+    local(4, 8)
+    across(0, C)
+    other_order = []
+    layer_sum()
+    local(8, 12)
+    line(2)
+    across(1, Y)
+    other(1, False)
+    local(12, 16)
+
+    def far0():
+        s_copy(ST, 0, st_bf.at[pl.ds(0, half)], b0.at[pl.ds(0, half)], to_core).wait_recv()
+        far(0, b0)
+
+    def far1():
+        from_core(B1C, b1)
+        far(1, b1)
+
+    def far2():
+        from_core(B2C, b2)
+        far(2, b2)
+
+    def far3():
+        from_core(B3C, b3)
+        far(3, b3)
+
+    pl.when(c == 1)(far0)
+    other(0, True)
+    across(1, C)
+    top_sum()
+    pl.when(x == 1)(far1)
+    line(3)
+    across(2, Y)
+    other(1, True)
+    other(2, False)
+    pl.when(lax.rem(z, 2) == 1)(far2)
+    across(2, C)
+    pl.when(z >= 2)(far3)
+
+    def norm_step(i, _):
+        for u in range(2):
+            h = i * 2 + u
+            m = mixed[:, lanes(h)]
+            inv = lax.rsqrt(jnp.mean(m * m, axis=1, keepdims=True) + 1e-06)
+            normed[:, lanes(h)] = (m * inv * gain_ref[:, lanes(h)]).astype(jnp.bfloat16)
+        return 0
+
+    lax.fori_loop(0, heads // 2, norm_step, 0)
+    across(3, Y)
+    other(2, True)
+    other(3, False)
+    across(3, C)
+    other(3, True)
+    loads[3].wait()
+
+    def partner(j, _):
+        shard = j * 2 + 1 - c
+        for n, size, start in ((0, part, 0), (1, rows - 2 * part, part), (2, part, rows - part)):
+            at = pl.ds(start, size)
+            pltpu.make_async_remote_copy(
+                src_ref=wbuf.at[shard, at], dst_ref=wbuf.at[shard, at],
+                send_sem=w_send.at[CORE, j, n], recv_sem=w_recv.at[shard, n],
+                device_id=to_core, device_id_type=MESH,
+            ).wait_recv()
+        return 0
+
+    lax.fori_loop(0, count // 2, partner, 0)
+
+    def project(j, _):
+        both_cols = jnp.concatenate([wbuf[2 * j], wbuf[2 * j + 1]], axis=1)
+        out_ref[:, pl.ds(pl.multiple_of(j * 2 * cols, 2 * cols), 2 * cols)] = jnp.dot(
+            normed[...], both_cols, preferred_element_type=jnp.float32
+        ).astype(jnp.bfloat16)
+        return 0
+
+    lax.fori_loop(0, count // 2, project, 0)
+
+    for cond, shard, which, way, is_own in sent:
+        under(cond, lambda: w_copy(shard, which, way, is_own).wait_send())
+    for cond, args in s_sent:
+        under(cond, lambda: s_copy(*args).wait_send())
+
+
+def kernel_body(queries, keys, values, level_index, level_table, norm_gain, out_weight):
+    stretch, width = queries.shape
+    table_rows, level_count, heads = level_table.shape
+    head_dim = width // heads
+    rows, cols = out_weight.shape
+    count = lax.axis_size("seq")
+    half = heads // 2
+    bf, f32 = jnp.bfloat16, jnp.float32
+    part = rows * 3 // 8
+    square = (head_dim, head_dim)
+    any_ = pl.BlockSpec(memory_space=pl.ANY)
+    vmem = pl.BlockSpec(memory_space=pltpu.VMEM)
+    return pl.pallas_call(
+        functools.partial(kernel, (count, 2, part)),
+        out_shape=jax.ShapeDtypeStruct((stretch, width), bf),
+        in_specs=[any_, any_, any_, vmem, vmem, vmem, any_],
+        out_specs=vmem,
+        scratch_shapes=[
+            pltpu.VMEM((stretch, width), bf),
+            pltpu.VMEM((stretch, width), bf),
+            pltpu.VMEM((stretch, width), bf),
+            pltpu.VMEM((count, rows, cols), bf),
+            pltpu.VMEM((heads, *square), f32),
+            pltpu.VMEM((heads, *square), bf),
+            pltpu.VMEM((heads, *square), bf),
+            pltpu.VMEM((heads, *square), bf),
+            pltpu.VMEM((heads, *square), bf),
+            pltpu.VMEM((heads, *square), bf),
+            pltpu.VMEM((half, *square), f32),
+            pltpu.VMEM((half, *square), bf),
+            pltpu.VMEM((half, *square), f32),
+            pltpu.VMEM((half, *square), bf),
+            pltpu.VMEM((stretch, width), f32),
+            pltpu.VMEM((stretch, width), bf),
+            pltpu.VMEM((heads, stretch, 128), f32),
+            pltpu.SemaphoreType.DMA((4,)),
+            pltpu.SemaphoreType.DMA((5, count // 2, 3)),
+            pltpu.SemaphoreType.DMA((count, 3)),
+            pltpu.SemaphoreType.DMA((7, 2)),
+            pltpu.SemaphoreType.DMA((7, 2)),
+        ],
+        compiler_params=pltpu.CompilerParams(collective_id=0, has_side_effects=True),
+    )(
+        queries, keys, values, level_index.reshape(1, stretch),
+        jnp.transpose(level_table, (2, 0, 1)), norm_gain.reshape(1, width), out_weight,
+    )
+
+
+def body(queries, keys, values, level_index, level_table, norm_gain, out_weight):
+    heads = level_table.shape[2]
+    fits = (
+        lax.axis_size("seq") == 1 << 4
+        and lax.axis_size("grp") == 2
+        and out_weight.shape[1] % 128 == 0
+        and queries.shape[1] // heads == 128
+        and heads % 4 == 0
+    )
+    run = kernel_body if fits else plain_body
+    return run(queries, keys, values, level_index, level_table, norm_gain, out_weight)
+
+
 def solution(mesh):
     placed = (
         P(("grp", "seq"), None),

time: 160 us -> 64.9 us (0.41)
  the two profiles are of different devices: /device:TPU:0 before, /device:TPU:27 now
where the time goes in v1:
time: 64.9 us; the launch traced here: 64.7 us
  Pallas kernels  60.5 us (93%)
  local copies, waits for them, and re-layouts  4.25 us (7%)
    pallas_call x1, Pallas kernels, kernel_body(): pl.pallas_call(functools.partial(kernel, (count, 2, part)), out_shape=jax...  60.5 us
    unnamed x2, local copies, waits for them, and re-layouts  4.25 us

profile of v1, /device:TPU:27, one launch (start us, length us, event | category | flops | bytes accessed | tf_op | source)
XLA Modules:
  0.0 64.7 jit_solution(9028135099926918063)
XLA Ops:
  0.0 1.9 %copy.8 = f32[64,18,16]{1,0,2:T(8,128)} copy(f32[64,18,16]{0,2,1:T(8,128)} %param.11) | data formatting | bytes 147456 | tf_op args[4]
  1.9 60.5 %shard_map.73 = bf16[256,2048]{1,0:T(8,128)(2,1)} custom-call(bf16[256,2048]{1,0:T(8,128)(2,1)} %q_hbm.1, bf16[256,2048]{1,0:T(8,128)(2,1)} %k_hbm.1, bf16[256,2048]{1,0:T(8,128)(2,1)} %v_hbm.1, s32[1,256]{1,0:T(1,128)} %bitcast.5, f32[16,64,18]{2,1,0:T(8,128)} %bitcast.3, f32[1,2048]{1,0:T(1,128)} %bitcast.4, bf16[2048,128]{1,0:T(8,128)(2,1)} %w_hbm.1), custom_call_target="tpu_custom_call" | custom-call | tf_op jit(solution)/shard_map/pallas_call | solution.py:530
  62.4 2.3 %copy.10 = bf16[256,2048]{1,0:T(8,128)(2,1)} copy(bf16[256,2048]{1,0:T(8,128)(2,1)} %shard_map.73) | data formatting | bytes 2097152

commit v2 on v1

--- a/solution.py
+++ b/solution.py
@@ -90,7 +90,7 @@
 ):
     count, ways, part = dims
     stretch, width = q.shape
-    heads, table_rows, level_count = tab_ref.shape
+    level_count, heads, table_rows = tab_ref.shape
     head_dim = width // heads
     half = heads // 2
     piece = half // 2
@@ -207,10 +207,16 @@
         shard = shard_of(jnp.where(ok, zz, z), x, c)
         arrive(ok, shard, which, side)
         send(both(ok, has_up if side == UP else has_down), shard, which, side)
-        send(ok, shard, which, ACROSS)
         if which == Y:
+            send(ok, shard, which, ACROSS)
             send(ok, shard, which, OTHER)
         send(ok, shard, which, CORE)
+
+    def late(d):
+        for side in (UP, DOWN):
+            zz = z - d if side == UP else z + d
+            ok = z >= d if side == UP else z + d < layers
+            send(ok, shard_of(jnp.where(ok, zz, z), x, c), C, ACROSS)
 
     def from_across(d, side, which):
         if d == 0:
@@ -234,10 +240,9 @@
         arrive(ok, shard, O, OTHER)
         send(ok, shard, O, CORE)
 
-    def line(d):
-        for which in (Y, C):
-            for side in (UP, DOWN):
-                from_line(d, side, which)
+    def line(d, which):
+        for side in (UP, DOWN):
+            from_line(d, side, which)
 
     def across(d, which):
         for side in (UP,) if d == 0 else (UP, DOWN):
@@ -292,7 +297,8 @@
     onehot = jnp.transpose(onehot_t, (1, 0)).astype(jnp.bfloat16)
 
     def lam_step(h, _):
-        full = tab_ref[h]
+        full = tab_ref[:, pl.ds(h, 1), :].reshape(level_count, table_rows)
+        full = jnp.transpose(full, (1, 0))
         hi = full.astype(jnp.bfloat16)
         rest = full - hi.astype(jnp.float32)
         mi = rest.astype(jnp.bfloat16)
@@ -413,11 +419,16 @@
 
     ps_bf2 = quad_bf
 
-    def top_sum():
+    def top_sum(layer):
+        there = z == layer
         for n in range(2):
-            pl.when(z >= 2)(lambda: s_copy(ZS, n, b3.at[own(n)], b3.at[own(n)], to_down).wait_recv())
-            s_start(z == 2, ZS, n, b3.at[own(n)], b3.at[own(n)], to_up)
-            s_start(z >= 2, B3C, n, b3.at[own(n)], b3.at[own(n)], to_core)
+            def arrived(n=n):
+                s_copy(ZS, n, b3.at[own(n)], b3.at[own(n)], to_down).wait_recv()
+
+            pl.when(there)(arrived)
+            if layer + 1 < layers:
+                s_start(there, ZS, n, b3.at[own(n)], b3.at[own(n)], to_up)
+            s_start(there, B3C, n, b3.at[own(n)], b3.at[own(n)], to_core)
 
     def theirs(n):
         return pl.ds(half - mine + n * piece, piece)
@@ -426,22 +437,6 @@
         for n in range(2):
             s_copy(kind, n, buf.at[theirs(n)], buf.at[theirs(n)], to_core).wait_recv()
 
-    chip_sum()
-    send(None, r, C, ACROSS, True)
-    local(0, 4)
-    line(1)
-    across(0, Y)
-    quad_sum()
-    local(4, 8)
-    across(0, C)
-    other_order = []
-    layer_sum()
-    local(8, 12)
-    line(2)
-    across(1, Y)
-    other(1, False)
-    local(12, 16)
-
     def far0():
         s_copy(ST, 0, st_bf.at[pl.ds(0, half)], b0.at[pl.ds(0, half)], to_core).wait_recv()
         far(0, b0)
@@ -457,19 +452,6 @@
     def far3():
         from_core(B3C, b3)
         far(3, b3)
-
-    pl.when(c == 1)(far0)
-    other(0, True)
-    across(1, C)
-    top_sum()
-    pl.when(x == 1)(far1)
-    line(3)
-    across(2, Y)
-    other(1, True)
-    other(2, False)
-    pl.when(lax.rem(z, 2) == 1)(far2)
-    across(2, C)
-    pl.when(z >= 2)(far3)
 
     def norm_step(i, _):
         for u in range(2):
@@ -479,35 +461,77 @@
             normed[:, lanes(h)] = (m * inv * gain_ref[:, lanes(h)]).astype(jnp.bfloat16)
         return 0
 
-    lax.fori_loop(0, heads // 2, norm_step, 0)
+    def partner(column):
+        def step(zz, _):
+            j = zz * 2 + column
+            shard = j * 2 + 1 - c
+            for n, size, start in ((0, part, 0), (1, rows - 2 * part, part), (2, part, rows - part)):
+                at = pl.ds(start, size)
+                pltpu.make_async_remote_copy(
+                    src_ref=wbuf.at[shard, at], dst_ref=wbuf.at[shard, at],
+                    send_sem=w_send.at[CORE, j, n], recv_sem=w_recv.at[shard, n],
+                    device_id=to_core, device_id_type=MESH,
+                ).wait_recv()
+            return 0
+
+        lax.fori_loop(0, layers, step, 0)
+
+    def project(column):
+        def step(zz, _):
+            j = zz * 2 + column
+            both_cols = jnp.concatenate([wbuf[2 * j], wbuf[2 * j + 1]], axis=1)
+            out_ref[:, pl.ds(pl.multiple_of(j * 2 * cols, 2 * cols), 2 * cols)] = jnp.dot(
+                normed[...], both_cols, preferred_element_type=jnp.float32
+            ).astype(jnp.bfloat16)
+            return 0
+
+        lax.fori_loop(0, layers, step, 0)
+
+    chip_sum()
+    across(0, Y)
+    line(1, Y)
+    local(0, 4)
+    line(1, C)
+    local(4, 6)
+    line(2, Y)
+    other(1, False)
+    quad_sum()
+    line(2, C)
+    send(None, r, C, ACROSS, True)
+    late(1)
+    other(0, True)
+    local(6, 8)
+    line(3, Y)
+    across(1, Y)
+    layer_sum()
+    line(3, C)
+    late(2)
+    late(3)
+    other(2, False)
+    across(2, Y)
+    local(8, 12)
+    top_sum(layers - 2)
+    other(1, True)
+    across(0, C)
+    local(12, 16)
+    pl.when(c == 1)(far0)
+    across(1, C)
+    other(3, False)
+    pl.when(x == 1)(far1)
     across(3, Y)
     other(2, True)
-    other(3, False)
+    top_sum(layers - 1)
+    pl.when(lax.rem(z, 2) == 1)(far2)
+    across(2, C)
+    pl.when(z >= 2)(far3)
+    lax.fori_loop(0, heads // 2, norm_step, 0)
+    loads[3].wait()
+    partner(x)
     across(3, C)
     other(3, True)
-    loads[3].wait()
-
-    def partner(j, _):
-        shard = j * 2 + 1 - c
-        for n, size, start in ((0, part, 0), (1, rows - 2 * part, part), (2, part, rows - part)):
-            at = pl.ds(start, size)
-            pltpu.make_async_remote_copy(
-                src_ref=wbuf.at[shard, at], dst_ref=wbuf.at[shard, at],
-                send_sem=w_send.at[CORE, j, n], recv_sem=w_recv.at[shard, n],
-                device_id=to_core, device_id_type=MESH,
-            ).wait_recv()
-        return 0
-
-    lax.fori_loop(0, count // 2, partner, 0)
-
-    def project(j, _):
-        both_cols = jnp.concatenate([wbuf[2 * j], wbuf[2 * j + 1]], axis=1)
-        out_ref[:, pl.ds(pl.multiple_of(j * 2 * cols, 2 * cols), 2 * cols)] = jnp.dot(
-            normed[...], both_cols, preferred_element_type=jnp.float32
-        ).astype(jnp.bfloat16)
-        return 0
-
-    lax.fori_loop(0, count // 2, project, 0)
+    project(x)
+    partner(1 - x)
+    project(1 - x)
 
     for cond, shard, which, way, is_own in sent:
         under(cond, lambda: w_copy(shard, which, way, is_own).wait_send())
@@ -559,7 +583,7 @@
         compiler_params=pltpu.CompilerParams(collective_id=0, has_side_effects=True),
     )(
         queries, keys, values, level_index.reshape(1, stretch),
-        jnp.transpose(level_table, (2, 0, 1)), norm_gain.reshape(1, width), out_weight,
+        jnp.transpose(level_table, (1, 2, 0)), norm_gain.reshape(1, width), out_weight,
     )
 
 

time: 64.9 us -> 54.9 us (0.85)
  Pallas kernels: 60.5 us -> 52.5 us
  local copies, waits for them, and re-layouts: 4.25 us -> 2.3 us
    pallas_call x1, Pallas kernels: 60.5 us -> 52.5 us  [kernel_body(): pl.pallas_call(functools.partial(kernel, (count, 2, part)), out_shape=jax...]
    unnamed x2 -> x1, local copies, waits for them, and re-layouts: 4.25 us -> 2.3 us
where the time goes in v2:
time: 54.9 us; the launch traced here: 54.8 us
  Pallas kernels  52.5 us (96%)
  local copies, waits for them, and re-layouts  2.3 us (4%)
    pallas_call x1, Pallas kernels, kernel_body(): pl.pallas_call(functools.partial(kernel, (count, 2, part)), out_shape=jax...  52.5 us
    unnamed x1, local copies, waits for them, and re-layouts  2.3 us

profile of v2, /device:TPU:27, one launch (start us, length us, event | category | flops | bytes accessed | tf_op | source)
XLA Modules:
  0.0 54.8 jit_solution(16353920266003116365)
XLA Ops:
  0.0 52.5 %shard_map.73 = bf16[256,2048]{1,0:T(8,128)(2,1)} custom-call(bf16[256,2048]{1,0:T(8,128)(2,1)} %q_hbm.1, bf16[256,2048]{1,0:T(8,128)(2,1)} %k_hbm.1, bf16[256,2048]{1,0:T(8,128)(2,1)} %v_hbm.1, s32[1,256]{1,0:T(1,128)} %bitcast.5, f32[18,16,64]{2,1,0:T(8,128)} %bitcast.3, f32[1,2048]{1,0:T(1,128)} %bitcast.4, bf16[2048,128]{1,0:T(8,128)(2,1)} %w_hbm.1), custom_call_target="tpu_custom_call" | custom-call | tf_op jit(solution)/shard_map/pallas_call | solution.py:554
  52.5 2.3 %copy.9 = bf16[256,2048]{1,0:T(8,128)(2,1)} copy(bf16[256,2048]{1,0:T(8,128)(2,1)} %shard_map.73) | data formatting | bytes 2097152

commit v3 on v2

--- a/solution.py
+++ b/solution.py
@@ -275,8 +275,8 @@
 
     def state_loop(first):
         def step(i, _):
-            for u in range(2):
-                h = first + i * 2 + u
+            for u in range(4):
+                h = first + i * 4 + u
                 one = lax.dot_general(
                     k[:, lanes(h)], v[:, lanes(h)], (((0,), (0,)), ((), ())),
                     preferred_element_type=jnp.float32,
@@ -285,7 +285,7 @@
                 st_bf[h] = one.astype(jnp.bfloat16)
             return 0
 
-        lax.fori_loop(0, half // 2, step, 0)
+        lax.fori_loop(0, half // 4, step, 0)
 
     state_loop(0)
     s_start(None, ST, 0, st_bf.at[pl.ds(0, half)], b0.at[pl.ds(0, half)], to_core)
@@ -296,20 +296,22 @@
     onehot_t = jnp.where(row_of == idx_ref[...], 1.0, 0.0)
     onehot = jnp.transpose(onehot_t, (1, 0)).astype(jnp.bfloat16)
 
-    def lam_step(h, _):
-        full = tab_ref[:, pl.ds(h, 1), :].reshape(level_count, table_rows)
-        full = jnp.transpose(full, (1, 0))
-        hi = full.astype(jnp.bfloat16)
-        rest = full - hi.astype(jnp.float32)
-        mi = rest.astype(jnp.bfloat16)
-        lo = (rest - mi.astype(jnp.float32)).astype(jnp.bfloat16)
-        total = jnp.dot(onehot, lo, preferred_element_type=jnp.float32)
-        total = total + jnp.dot(onehot, mi, preferred_element_type=jnp.float32)
-        total = total + jnp.dot(onehot, hi, preferred_element_type=jnp.float32)
-        lam[h, :, pl.ds(0, level_count)] = total
+    def lam_step(i, _):
+        for u in range(4):
+            h = i * 4 + u
+            full = tab_ref[:, pl.ds(h, 1), :].reshape(level_count, table_rows)
+            full = jnp.transpose(full, (1, 0))
+            hi = full.astype(jnp.bfloat16)
+            rest = full - hi.astype(jnp.float32)
+            mi = rest.astype(jnp.bfloat16)
+            lo = (rest - mi.astype(jnp.float32)).astype(jnp.bfloat16)
+            total = jnp.dot(onehot, lo, preferred_element_type=jnp.float32)
+            total = total + jnp.dot(onehot, mi, preferred_element_type=jnp.float32)
+            total = total + jnp.dot(onehot, hi, preferred_element_type=jnp.float32)
+            lam[h, :, pl.ds(0, level_count)] = total
         return 0
 
-    lax.fori_loop(0, heads, lam_step, 0)
+    lax.fori_loop(0, heads // 4, lam_step, 0)
 
     ti = lax.broadcasted_iota(jnp.int32, (mid, mid), 0)
     si = lax.broadcasted_iota(jnp.int32, (mid, mid), 1)
@@ -356,15 +358,15 @@
 
     def far(bit, bucket):
         def step(i, _):
-            for u in range(2):
-                h = i * 2 + u
+            for u in range(4):
+                h = i * 4 + u
                 term = jnp.dot(q[:, lanes(h)], bucket[h], preferred_element_type=jnp.float32)
                 level = log_stretch + 1 + bit
                 weight = lam[h][:, level : level + 1]
                 mixed[:, lanes(h)] = mixed[:, lanes(h)] + weight * term * scale
             return 0
 
-        lax.fori_loop(0, heads // 2, step, 0)
+        lax.fori_loop(0, heads // 4, step, 0)
 
     def own(n):
         return pl.ds(mine + n * piece, piece)
@@ -454,8 +456,8 @@
         far(3, b3)
 
     def norm_step(i, _):
-        for u in range(2):
-            h = i * 2 + u
+        for u in range(4):
+            h = i * 4 + u
             m = mixed[:, lanes(h)]
             inv = lax.rsqrt(jnp.mean(m * m, axis=1, keepdims=True) + 1e-06)
             normed[:, lanes(h)] = (m * inv * gain_ref[:, lanes(h)]).astype(jnp.bfloat16)
@@ -524,7 +526,7 @@
     pl.when(lax.rem(z, 2) == 1)(far2)
     across(2, C)
     pl.when(z >= 2)(far3)
-    lax.fori_loop(0, heads // 2, norm_step, 0)
+    lax.fori_loop(0, heads // 4, norm_step, 0)
     loads[3].wait()
     partner(x)
     across(3, C)

time: 54.9 us -> 52.3 us (0.953)
  Pallas kernels: 52.5 us -> 49.9 us
    pallas_call x1, Pallas kernels: 52.5 us -> 49.9 us  [kernel_body(): pl.pallas_call(functools.partial(kernel, (count, 2, part)), out_shape=jax...]
where the time goes in v3:
time: 52.3 us; the launch traced here: 52.2 us
  Pallas kernels  49.9 us (95%)
  local copies, waits for them, and re-layouts  2.3 us (4%)
    pallas_call x1, Pallas kernels, kernel_body(): pl.pallas_call(functools.partial(kernel, (count, 2, part)), out_shape=jax...  49.9 us
    unnamed x1, local copies, waits for them, and re-layouts  2.3 us

profile of v3, /device:TPU:27, one launch (start us, length us, event | category | flops | bytes accessed | tf_op | source)
XLA Modules:
  0.0 52.2 jit_solution(7399696549393529611)
XLA Ops:
  0.0 49.9 %shard_map.73 = bf16[256,2048]{1,0:T(8,128)(2,1)} custom-call(bf16[256,2048]{1,0:T(8,128)(2,1)} %q_hbm.1, bf16[256,2048]{1,0:T(8,128)(2,1)} %k_hbm.1, bf16[256,2048]{1,0:T(8,128)(2,1)} %v_hbm.1, s32[1,256]{1,0:T(1,128)} %bitcast.5, f32[18,16,64]{2,1,0:T(8,128)} %bitcast.3, f32[1,2048]{1,0:T(1,128)} %bitcast.4, bf16[2048,128]{1,0:T(8,128)(2,1)} %w_hbm.1), custom_call_target="tpu_custom_call" | custom-call | tf_op jit(solution)/shard_map/pallas_call | solution.py:556
  49.9 2.3 %copy.9 = bf16[256,2048]{1,0:T(8,128)(2,1)} copy(bf16[256,2048]{1,0:T(8,128)(2,1)} %shard_map.73) | data formatting | bytes 2097152
